TPU v7x, 128 devices: a whole 4x4x4 slice. The times are simulated.
128 devices in a mesh: smp: 8 (over y, core), gx: 8 (over z_lo, x), gz: 2 (over z_hi).
Axes of the slice: x: 4, y: 4, z: 4 (z_hi: 2, z_lo: 2; z = z_hi * 2 + z_lo), core: 2. Of those that a mesh axis runs over, the one named last changes fastest.
Arguments:
- features: bfloat16 [8, 32, 40, 8, 256], P('smp', None, 'gx', None, 'gz'), may hold values from -6 to 6
- first_weight: bfloat16 [32, 3, 3, 3, 32], replicated, may hold values from -0.21875 to 0.21875
- first_bias: float32 [32], replicated, may hold values from -1 to 1
- second_weight: bfloat16 [32, 3, 3, 3, 32], replicated, may hold values from -0.21875 to 0.21875
- second_bias: float32 [32], replicated, may hold values from -1 to 1
- cotangent: bfloat16 [8, 32, 40, 8, 256], P('smp', None, 'gx', None, 'gz'), may hold values from -6 to 6
Outputs:
- output: bfloat16 [8, 32, 40, 8, 256], P('smp', None, 'gx', None, 'gz')
- first_grad: float32 [32, 3, 3, 3, 32], replicated
- first_bias_grad: float32 [32], replicated
- second_grad: float32 [32, 3, 3, 3, 32], replicated
- second_bias_grad: float32 [32], replicated
All inputs are finite; a program needn't handle non-finite values.
Results may differ from a plain program's by a relative error of at most 0.011.
Values may be sent and summed in bfloat16 or wider, within the bound.
A program may use at most 128 MiB of HBM per device.

v0:
```python
import jax
import jax.numpy as jnp
from jax import lax
from jax.sharding import PartitionSpec as P


def extended(array, sides, width):
    for axis, dim in sides:
        size, length = (lax.axis_size(axis), array.shape[dim])
        up = [(i, (i + 1) % size) for i in range(size)]
        down = [(j, i) for i, j in up]
        last = lax.slice_in_dim(array, length - width, length, axis=dim)
        initial = lax.slice_in_dim(array, 0, width, axis=dim)
        before = lax.ppermute(last, axis, up)
        after = lax.ppermute(initial, axis, down)
        array = jnp.concatenate([before, array, after], axis=dim)
    return array


def wall_pad(field_in):
    return jnp.pad(field_in, ((0, 0), (0, 0), (0, 0), (1, 1), (0, 0)))


def extend(field_in, depth_cells):
    both_wide = extended(field_in, (("gx", 2), ("gz", 4)), depth_cells)
    return wall_pad(both_wide)


def stack_taps(padded, offset_x, offset_y, cells_x, cells_y, cells_z):
    return jnp.concatenate(
        [
            padded[
                :,
                :,
                offset_x : offset_x + cells_x,
                offset_y : offset_y + cells_y,
                offset_z : offset_z + cells_z,
            ]
            for offset_z in range(3)
        ],
        axis=1,
    )


def convolve(padded, weight):
    cells_x = padded.shape[2] - 2
    cells_y = padded.shape[3] - 2
    cells_z = padded.shape[4] - 2
    summed = jnp.zeros((padded.shape[0], weight.shape[0], cells_x, cells_y, cells_z), jnp.float32)
    for offset_x in range(3):
        for offset_y in range(3):
            stacked = stack_taps(padded, offset_x, offset_y, cells_x, cells_y, cells_z)
            tap_block = weight[:, offset_x, offset_y].reshape(weight.shape[0], -1)
            summed = summed + jnp.einsum(
                "ok,skxyz->soxyz", tap_block, stacked, preferred_element_type=jnp.float32
            )
    return summed


def correlate(upstream, padded):
    cells_x = upstream.shape[2]
    cells_y = upstream.shape[3]
    cells_z = upstream.shape[4]
    outer_terms = []
    for offset_x in range(3):
        inner_terms = []
        for offset_y in range(3):
            stacked = stack_taps(padded, offset_x, offset_y, cells_x, cells_y, cells_z)
            local_term = jnp.einsum(
                "soxyz,skxyz->ok", upstream, stacked, preferred_element_type=jnp.float32
            )
            inner_terms.append(local_term.reshape(upstream.shape[1], 3, -1))
        outer_terms.append(jnp.stack(inner_terms, axis=1))
    return jnp.stack(outer_terms, axis=1)


def shards(features, first_weight, first_bias, second_weight, second_bias, cotangent):
    input_pad = extend(features, 1)
    preact = convolve(input_pad, first_weight) + first_bias[None, :, None, None, None]
    hidden = jax.nn.silu(preact).astype(jnp.bfloat16)
    hidden_pad = extend(hidden, 1)
    residual_term = convolve(hidden_pad, second_weight) + second_bias[None, :, None, None, None]
    output = (features.astype(jnp.float32) + residual_term).astype(jnp.bfloat16)
    cells_all = (
        features.shape[0]
        * lax.axis_size("smp")
        * features.shape[2]
        * lax.axis_size("gx")
        * features.shape[3]
        * features.shape[4]
        * lax.axis_size("gz")
    )
    grad_scale = 1.0 / cells_all**0.5
    second_grad = correlate(cotangent, hidden_pad) * grad_scale
    second_bgrad = jnp.sum(cotangent, axis=(0, 2, 3, 4), dtype=jnp.float32) * grad_scale
    flipped = jnp.transpose(jnp.flip(second_weight, (1, 2, 3)), (4, 1, 2, 3, 0))
    upstream_pad = extend(cotangent, 1)
    hidden_grad = convolve(upstream_pad, flipped)
    logistic = jax.nn.sigmoid(preact)
    preact_grad = (hidden_grad * logistic * (1.0 + preact * (1.0 - logistic))).astype(jnp.bfloat16)
    first_grad = correlate(preact_grad, input_pad) * grad_scale
    first_bgrad = jnp.sum(preact_grad, axis=(0, 2, 3, 4), dtype=jnp.float32) * grad_scale
    first_grad, first_bgrad, second_grad, second_bgrad = lax.psum(
        (first_grad, first_bgrad, second_grad, second_bgrad), ("smp", "gx", "gz")
    )
    return (output, first_grad, first_bgrad, second_grad, second_bgrad)


def solution(mesh):
    in_specs = (
        P("smp", None, "gx", None, "gz"),
        P(),
        P(),
        P(),
        P(),
        P("smp", None, "gx", None, "gz"),
    )
    out_specs = (P("smp", None, "gx", None, "gz"), P(), P(), P(), P())
    return jax.shard_map(shards, mesh=mesh, in_specs=in_specs, out_specs=out_specs, check_vma=False)
```

profile of v0, /device:TPU:1, one launch (start us, length us, event | category | flops | bytes accessed | tf_op | source)
XLA Modules:
  0.0 336.7 jit_solution(1771370892015134245)
XLA Ops:
  7.2 1.1 copy.113
  8.3 4.7 %collective-permute-start.9 = (bf16[1,32,1,8,128]{4,1,3,2,0:T(8,128)(2,1)S(1)}, bf16[1,32,1,8,128]{4,1,3,2,0:T(8,128)(2,1)S(1)}, u32[]{:S(2)}, u32[]{:S(2)}) collective-permute-start(bf16[1,32,1,8,128]{4,1,3,2,0:T(8,128)(2,1)S(1)} %get-tuple-element.105), channel_id=1, source_target_pairs={{2,0},{4,2},{6,4},{8,6},{10,8},{12,10},{14,12},{0,14},{3,1},{5,3},... | collective-permute-start | bytes 196616 | tf_op jit(solution)/shard_map/ppermute | solution.py:15
  13.1 1.1 copy.88
  14.2 3.6 %collective-permute-start.1 = (bf16[1,32,1,8,128]{4,1,3,2,0:T(8,128)(2,1)S(1)}, bf16[1,32,1,8,128]{4,1,3,2,0:T(8,128)(2,1)S(1)}, u32[]{:S(2)}, u32[]{:S(2)}) collective-permute-start(bf16[1,32,1,8,128]{4,1,3,2,0:T(8,128)(2,1)S(1)} %get-tuple-element.109), channel_id=1, source_target_pairs={{2,0},{4,2},{6,4},{8,6},{10,8},{12,10},{14,12},{0,14},{3,1},{5,3},... | collective-permute-start | bytes 196616 | tf_op jit(solution)/shard_map/ppermute | solution.py:15
  17.8 0.3 convert_reduce_fusion
  20.6 2.4 collective-permute-done
  23.1 3.4 %collective-permute-start.10 = (bf16[1,32,7,8,1]{4,1,3,2,0:T(8,128)(2,1)S(1)}, bf16[1,32,7,8,1]{4,1,3,2,0:T(8,128)(2,1)S(1)}, u32[]{:S(2)}, u32[]{:S(2)}) collective-permute-start(bf16[1,32,7,8,1]{4,1,3,2,0:T(8,128)(2,1)S(1)} %get-tuple-element.89), channel_id=1, source_target_pairs={{0,1},{1,0},{2,3},{3,2},{4,5},{5,4},{6,7},{7,6},{8,9},{9,8},{10,11... | collective-permute-start | bytes 10760 | tf_op jit(solution)/shard_map/ppermute | solution.py:14
  26.8 3.0 collective-permute-start.2
  29.8 4.7 %collective-permute-done.10 = bf16[1,32,7,8,1]{4,1,3,2,0:T(8,128)(2,1)S(1)} collective-permute-done((bf16[1,32,7,8,1]{4,1,3,2,0:T(8,128)(2,1)S(1)}, bf16[1,32,7,8,1]{4,1,3,2,0:T(8,128)(2,1)S(1)}, u32[]{:S(2)}, u32[]{:S(2)}) %collective-permute-start.10) | collective-permute-done | bytes 3616 | tf_op jit(solution)/shard_map/ppermute | solution.py:14
  34.5 9.8 %collective-permute-done.11 = bf16[1,32,7,8,1]{4,1,3,2,0:T(8,128)(2,1)S(1)} collective-permute-done((bf16[1,32,7,8,1]{4,1,3,2,0:T(8,128)(2,1)S(1)}, bf16[1,32,7,8,1]{4,1,3,2,0:T(8,128)(2,1)S(1)}, u32[]{:S(2)}, u32[]{:S(2)}) %collective-permute-start.11) | collective-permute-done | bytes 3616 | tf_op jit(solution)/shard_map/ppermute | solution.py:15
  44.4 0.6 select_maximum_fusion
  44.9 1.5 fusion.148
  46.5 7.7 %collective-permute-done.2 = bf16[1,32,7,8,1]{4,1,3,2,0:T(8,128)(2,1)S(1)} collective-permute-done((bf16[1,32,7,8,1]{4,1,3,2,0:T(8,128)(2,1)S(1)}, bf16[1,32,7,8,1]{4,1,3,2,0:T(8,128)(2,1)S(1)}, u32[]{:S(2)}, u32[]{:S(2)}) %collective-permute-start.2) | collective-permute-done | bytes 3616 | tf_op jit(solution)/shard_map/ppermute | solution.py:14
  54.2 9.8 %collective-permute-done.3 = bf16[1,32,7,8,1]{4,1,3,2,0:T(8,128)(2,1)S(1)} collective-permute-done((bf16[1,32,7,8,1]{4,1,3,2,0:T(8,128)(2,1)S(1)}, bf16[1,32,7,8,1]{4,1,3,2,0:T(8,128)(2,1)S(1)}, u32[]{:S(2)}, u32[]{:S(2)}) %collective-permute-start.3) | collective-permute-done | bytes 3616 | tf_op jit(solution)/shard_map/ppermute | solution.py:15
  64.0 0.6 fusion.20
  64.6 1.5 fusion.150
  66.4 0.6 fusion.101
  67.1 1.1 pad_maximum_fusion.14
  70.6 0.5 copy-done.5
  71.1 0.3 multiply_convert_fusion
  71.4 0.3 fusion.44
  71.7 0.6 fusion.97
  72.4 0.3 convolution_add_fusion.7
  72.7 0.3 convolution_add_fusion.6
  73.0 0.3 convolution_add_fusion.5
  73.3 0.3 convolution_add_fusion.4
  73.6 0.3 convolution_add_fusion.3
  73.9 0.3 convolution_add_fusion.2
  74.2 1.0 convolution_add_fusion.1
  75.3 0.6 convert_reduce_fusion.1
  75.9 0.7 convolution_bitcast_fusion.6
  76.6 0.7 convolution_bitcast_fusion.5
  77.3 0.7 convolution_bitcast_fusion.4
  78.0 0.7 convolution_bitcast_fusion.3
  78.7 0.7 convolution_bitcast_fusion.1
  79.4 0.7 convolution_bitcast_fusion.7
  80.1 0.7 convolution_bitcast_fusion.8
  80.9 0.7 convolution_bitcast_fusion.2
  81.6 0.7 convolution_bitcast_fusion
  82.4 3.6 %collective-permute-start.5 = (bf16[1,32,1,8,128]{4,1,3,2,0:T(8,128)(2,1)S(1)}, bf16[1,32,1,8,128]{4,1,3,2,0:T(8,128)(2,1)S(1)}, u32[]{:S(2)}, u32[]{:S(2)}) collective-permute-start(bf16[1,32,1,8,128]{4,1,3,2,0:T(8,128)(2,1)S(1)} %get-tuple-element.108), channel_id=1, source_target_pairs={{2,0},{4,2},{6,4},{8,6},{10,8},{12,10},{14,12},{0,14},{3,1},{5,3},... | collective-permute-start | bytes 196616 | tf_op jit(solution)/shard_map/ppermute | solution.py:15
  86.0 1.6 collective-permute-done.4
  87.9 2.8 collective-permute-start.6
  90.7 0.3 collective-permute-start.7
  91.0 0.8 maximum_multiply_fusion
  91.8 78.4 %all-reduce.3 = (f32[32]{0:T(128)}, f32[32]{0:T(128)}) all-reduce(f32[32]{0:T(128)S(1)} %broadcast_multiply_fusion.1, f32[32]{0:T(128)S(1)} %broadcast_multiply_fusion), channel_id=1, replica_groups=mesh['smp'=8,'gx'=8,'gz'=2] {'smp','gx','gz'}, use_global_device_ids=true, to_apply=%region_2.3 | all-reduce | flops 64 | bytes 512 | tf_op jit(solution)/shard_map/psum | solution.py:103
  170.1 0.7 maximum_maximum_fusion
  170.9 0.5 fusion.151
  171.3 0.4 pad_maximum_fusion.21
  171.7 0.7 convolution_bitcast_fusion.13
  172.4 0.7 convolution_bitcast_fusion.10
  173.1 0.7 convolution_bitcast_fusion.16
  173.8 0.6 select_maximum_fusion.2
  174.4 1.4 fusion.149
  176.0 0.7 convolution_bitcast_fusion.11
  176.7 0.7 convolution_bitcast_fusion.9
  177.7 0.7 convolution_bitcast_fusion.14
  178.4 0.7 convolution_bitcast_fusion.12
  179.6 0.7 convolution_bitcast_fusion.17
  180.3 0.7 convolution_bitcast_fusion.15
  183.0 0.8 maximum_multiply_fusion.1
  184.1 0.9 copy.164
  185.0 142.2 %all-reduce.7.cloned.1.call-done = (f32[32,3,3,3,32]{4,0,3,2,1:T(8,128)}, f32[32,3,3,3,32]{4,0,3,2,1:T(8,128)}) async-done(((f32[32,3,3,3,32]{4,0,3,2,1:T(8,128)}, f32[32,3,3,3,32]{4,0,3,2,1:T(8,128)}), (f32[32,3,3,3,32]{4,0,3,2,1:T(8,128)}, f32[32,3,3,3,32]{4,0,3,2,1:T(8,128)})) %all-reduce.7.cloned.1.call-update) | async-done | bytes 221200 | tf_op jit(solution)/shard_map/psum | solution.py:103
  327.2 1.9 copy.328
  329.1 0.8 copy.329
  (110 shorter events, 9.2 us)
Async XLA Ops:
  7.2 10.6 %copy-start = (bf16[1,32,5,8,128]{4,3,2,1,0:T(8,128)(2,1)S(1)}, bf16[1,32,5,8,128]{4,3,2,1,0:T(8,128)(2,1)}, u32[]{:S(2)}) copy-start(bf16[1,32,5,8,128]{4,3,2,1,0:T(8,128)(2,1)} %param.11) | copy-start | bytes 983044
  7.2 10.9 %copy-start.2 = (bf16[32,3,3,3,32]{4,0,3,2,1:T(8,128)(2,1)S(1)}, bf16[32,3,3,3,32]{4,0,3,2,1:T(8,128)(2,1)}, u32[]{:S(2)}) copy-start(bf16[32,3,3,3,32]{4,0,3,2,1:T(8,128)(2,1)} %param.9) | copy-start | bytes 165892
  7.2 320.0 %all-reduce.7.cloned.1.call-start = ((), (), s32[]{:S(2)}) async-start(), calls=%async_computation | async-start | bytes 1769472 | tf_op jit(solution)/shard_map/psum | solution.py:103
  8.3 12.0 %collective-permute-start.9 = (bf16[1,32,1,8,128]{4,1,3,2,0:T(8,128)(2,1)S(1)}, bf16[1,32,1,8,128]{4,1,3,2,0:T(8,128)(2,1)S(1)}, u32[]{:S(2)}, u32[]{:S(2)}) collective-permute-start(bf16[1,32,1,8,128]{4,1,3,2,0:T(8,128)(2,1)S(1)} %get-tuple-element.105), channel_id=1, source_target_pairs={{2,0},{4,2},{6,4},{8,6},{10,8},{12,10},{14,12},{0,14},{3,1},{5,3},... | collective-permute-start | bytes 196616 | tf_op jit(solution)/shard_map/ppermute | solution.py:15
  13.1 5.1 %copy-start.4 = (bf16[32,3,3,3,32]{4,0,3,2,1:T(8,128)(2,1)S(1)}, bf16[32,3,3,3,32]{4,0,3,2,1:T(8,128)(2,1)}, u32[]{:S(2)}) copy-start(bf16[32,3,3,3,32]{4,0,3,2,1:T(8,128)(2,1)} %param.7) | copy-start | bytes 165892
  13.1 7.2 %collective-permute-start.8 = (bf16[1,32,1,8,128]{4,1,3,2,0:T(8,128)(2,1)S(1)}, bf16[1,32,1,8,128]{4,1,3,2,0:T(8,128)(2,1)S(1)}, u32[]{:S(2)}, u32[]{:S(2)}) collective-permute-start(bf16[1,32,1,8,128]{4,1,3,2,0:T(8,128)(2,1)S(1)} %get-tuple-element.106), channel_id=1, source_target_pairs={{0,2},{2,4},{4,6},{6,8},{8,10},{10,12},{12,14},{14,0},{1,3},{3,5},... | collective-permute-start | bytes 196616 | tf_op jit(solution)/shard_map/ppermute | solution.py:14
  14.2 12.4 %collective-permute-start.1 = (bf16[1,32,1,8,128]{4,1,3,2,0:T(8,128)(2,1)S(1)}, bf16[1,32,1,8,128]{4,1,3,2,0:T(8,128)(2,1)S(1)}, u32[]{:S(2)}, u32[]{:S(2)}) collective-permute-start(bf16[1,32,1,8,128]{4,1,3,2,0:T(8,128)(2,1)S(1)} %get-tuple-element.109), channel_id=1, source_target_pairs={{2,0},{4,2},{6,4},{8,6},{10,8},{12,10},{14,12},{0,14},{3,1},{5,3},... | collective-permute-start | bytes 196616 | tf_op jit(solution)/shard_map/ppermute | solution.py:15
  17.8 5.2 %collective-permute-start = (bf16[1,32,1,8,128]{4,1,3,2,0:T(8,128)(2,1)S(1)}, bf16[1,32,1,8,128]{4,1,3,2,0:T(8,128)(2,1)S(1)}, u32[]{:S(2)}, u32[]{:S(2)}) collective-permute-start(bf16[1,32,1,8,128]{4,1,3,2,0:T(8,128)(2,1)S(1)} %get-tuple-element.110), channel_id=1, source_target_pairs={{0,2},{2,4},{4,6},{6,8},{8,10},{10,12},{12,14},{14,0},{1,3},{3,5},... | collective-permute-start | bytes 196616 | tf_op jit(solution)/shard_map/ppermute | solution.py:14
  20.3 2.7 copy-start.1
  23.1 11.4 %collective-permute-start.10 = (bf16[1,32,7,8,1]{4,1,3,2,0:T(8,128)(2,1)S(1)}, bf16[1,32,7,8,1]{4,1,3,2,0:T(8,128)(2,1)S(1)}, u32[]{:S(2)}, u32[]{:S(2)}) collective-permute-start(bf16[1,32,7,8,1]{4,1,3,2,0:T(8,128)(2,1)S(1)} %get-tuple-element.89), channel_id=1, source_target_pairs={{0,1},{1,0},{2,3},{3,2},{4,5},{5,4},{6,7},{7,6},{8,9},{9,8},{10,11... | collective-permute-start | bytes 10760 | tf_op jit(solution)/shard_map/ppermute | solution.py:14
  26.5 17.9 %collective-permute-start.11 = (bf16[1,32,7,8,1]{4,1,3,2,0:T(8,128)(2,1)S(1)}, bf16[1,32,7,8,1]{4,1,3,2,0:T(8,128)(2,1)S(1)}, u32[]{:S(2)}, u32[]{:S(2)}) collective-permute-start(bf16[1,32,7,8,1]{4,1,3,2,0:T(8,128)(2,1)S(1)} %get-tuple-element.90), channel_id=1, source_target_pairs={{1,0},{0,1},{3,2},{2,3},{5,4},{4,5},{7,6},{6,7},{9,8},{8,9},{11,10... | collective-permute-start | bytes 10760 | tf_op jit(solution)/shard_map/ppermute | solution.py:15
  26.8 27.4 %collective-permute-start.2 = (bf16[1,32,7,8,1]{4,1,3,2,0:T(8,128)(2,1)S(1)}, bf16[1,32,7,8,1]{4,1,3,2,0:T(8,128)(2,1)S(1)}, u32[]{:S(2)}, u32[]{:S(2)}) collective-permute-start(bf16[1,32,7,8,1]{4,1,3,2,0:T(8,128)(2,1)S(1)} %get-tuple-element.97), channel_id=1, source_target_pairs={{0,1},{1,0},{2,3},{3,2},{4,5},{5,4},{6,7},{7,6},{8,9},{9,8},{10,11... | collective-permute-start | bytes 10760 | tf_op jit(solution)/shard_map/ppermute | solution.py:14
  29.8 34.3 %collective-permute-start.3 = (bf16[1,32,7,8,1]{4,1,3,2,0:T(8,128)(2,1)S(1)}, bf16[1,32,7,8,1]{4,1,3,2,0:T(8,128)(2,1)S(1)}, u32[]{:S(2)}, u32[]{:S(2)}) collective-permute-start(bf16[1,32,7,8,1]{4,1,3,2,0:T(8,128)(2,1)S(1)} %get-tuple-element.98), channel_id=1, source_target_pairs={{1,0},{0,1},{3,2},{2,3},{5,4},{4,5},{7,6},{6,7},{9,8},{8,9},{11,10... | collective-permute-start | bytes 10760 | tf_op jit(solution)/shard_map/ppermute | solution.py:15
  70.4 0.7 copy-start.5
  82.3 5.3 %collective-permute-start.4 = (bf16[1,32,1,8,128]{4,1,3,2,0:T(8,128)(2,1)S(1)}, bf16[1,32,1,8,128]{4,1,3,2,0:T(8,128)(2,1)S(1)}, u32[]{:S(2)}, u32[]{:S(2)}) collective-permute-start(bf16[1,32,1,8,128]{4,1,3,2,0:T(8,128)(2,1)S(1)} %get-tuple-element.107), channel_id=1, source_target_pairs={{0,2},{2,4},{4,6},{6,8},{8,10},{10,12},{12,14},{14,0},{1,3},{3,5},... | collective-permute-start | bytes 196616 | tf_op jit(solution)/shard_map/ppermute | solution.py:14
  82.4 5.2 %collective-permute-start.5 = (bf16[1,32,1,8,128]{4,1,3,2,0:T(8,128)(2,1)S(1)}, bf16[1,32,1,8,128]{4,1,3,2,0:T(8,128)(2,1)S(1)}, u32[]{:S(2)}, u32[]{:S(2)}) collective-permute-start(bf16[1,32,1,8,128]{4,1,3,2,0:T(8,128)(2,1)S(1)} %get-tuple-element.108), channel_id=1, source_target_pairs={{2,0},{4,2},{6,4},{8,6},{10,8},{12,10},{14,12},{0,14},{3,1},{5,3},... | collective-permute-start | bytes 196616 | tf_op jit(solution)/shard_map/ppermute | solution.py:15
  87.9 82.2 %collective-permute-start.6 = (bf16[1,32,7,8,1]{4,1,3,2,0:T(8,128)(2,1)S(1)}, bf16[1,32,7,8,1]{4,1,3,2,0:T(8,128)(2,1)S(1)}, u32[]{:S(2)}, u32[]{:S(2)}) collective-permute-start(bf16[1,32,7,8,1]{4,1,3,2,0:T(8,128)(2,1)S(1)} %get-tuple-element.93), channel_id=1, source_target_pairs={{0,1},{1,0},{2,3},{3,2},{4,5},{5,4},{6,7},{7,6},{8,9},{9,8},{10,11... | collective-permute-start | bytes 10760 | tf_op jit(solution)/shard_map/ppermute | solution.py:14
  90.7 79.5 %collective-permute-start.7 = (bf16[1,32,7,8,1]{4,1,3,2,0:T(8,128)(2,1)S(1)}, bf16[1,32,7,8,1]{4,1,3,2,0:T(8,128)(2,1)S(1)}, u32[]{:S(2)}, u32[]{:S(2)}) collective-permute-start(bf16[1,32,7,8,1]{4,1,3,2,0:T(8,128)(2,1)S(1)} %get-tuple-element.94), channel_id=1, source_target_pairs={{1,0},{0,1},{3,2},{2,3},{5,4},{4,5},{7,6},{6,7},{9,8},{8,9},{11,10... | collective-permute-start | bytes 10760 | tf_op jit(solution)/shard_map/ppermute | solution.py:15
  182.9 0.9 copy-start.6
  327.2 1.9 copy-start.3
Sparse Core Ops, SparseCore 0:
  184.0 143.2 all-reduce.6
where the time goes:
time: 337 us
  waiting for transfers between devices  178 us (53%)
  blocking collectives  78.4 us (23%)
  starting transfers between devices  21.6 us (6%)
  matrix products  21.5 us (6%)
  between operations  14.6 us (4%)
  local copies, waits for them, and re-layouts  14 us (4%)
  other arithmetic  8.32 us (2%)
    psum x1, waiting for transfers between devices, shards(): lax.psum((first_grad, first_bgrad, second_grad, second_bgrad), ('smp', 'g...  142 us
    psum x1, blocking collectives, shards(): lax.psum((first_grad, first_bgrad, second_grad, second_bgrad), ('smp', 'g...  78.4 us
    ppermute x6, waiting for transfers between devices, extended(): after = lax.ppermute(initial, axis, down)  19.7 us
    ppermute x6, waiting for transfers between devices, extended(): before = lax.ppermute(last, axis, up)  16.3 us
    dot_general x18, matrix products, correlate(): jnp.einsum('soxyz,skxyz->ok', upstream, stacked, preferred_element_type=j...  12.8 us
    ppermute x6, starting transfers between devices, extended(): after = lax.ppermute(initial, axis, down)  12.4 us
    ppermute x6, starting transfers between devices, extended(): before = lax.ppermute(last, axis, up)  9.18 us
    dot_general x27, matrix products, convolve(): jnp.einsum('ok,skxyz->soxyz', tap_block, stacked, preferred_element_type=...  8.76 us
  transfers between devices with their start and end apart: 13, of which 7 were waited for; matrix products, arithmetic and copies ran while one was open for 2% of the time, Pallas kernels for 0%

commit v1 on v0

--- a/solution.py
+++ b/solution.py
@@ -2,6 +2,11 @@
 import jax.numpy as jnp
 from jax import lax
 from jax.sharding import PartitionSpec as P
+
+
+def one_after_other(array_2, first, second):
+    partial = lax.psum(array_2, first)
+    return lax.psum(partial, second)
 
 
 def extended(array, sides, width):
@@ -100,8 +105,8 @@
     preact_grad = (hidden_grad * logistic * (1.0 + preact * (1.0 - logistic))).astype(jnp.bfloat16)
     first_grad = correlate(preact_grad, input_pad) * grad_scale
     first_bgrad = jnp.sum(preact_grad, axis=(0, 2, 3, 4), dtype=jnp.float32) * grad_scale
-    first_grad, first_bgrad, second_grad, second_bgrad = lax.psum(
-        (first_grad, first_bgrad, second_grad, second_bgrad), ("smp", "gx", "gz")
+    first_grad, first_bgrad, second_grad, second_bgrad = one_after_other(
+        (first_grad, first_bgrad, second_grad, second_bgrad), ("gx", "gz"), "smp"
     )
     return (output, first_grad, first_bgrad, second_grad, second_bgrad)
 

time: 337 us -> 325 us (0.964)
  blocking collectives: 78.4 us -> 65.8 us
  waiting for transfers between devices: 178 us -> 173 us
  matrix products: 21.5 us -> 25.4 us
    psum x1 -> x2, blocking collectives: 78.4 us -> 65.8 us  [the longest x1 41 us: one_after_other(): partial = lax.psum(array_2, first)]
    psum x1 -> x2, waiting for transfers between devices: 142 us -> 137 us  [the longest x1 76.7 us: one_after_other(): partial = lax.psum(array_2, first)]
    dot_general x27, matrix products: 8.76 us -> 12.6 us  [convolve(): jnp.einsum('ok,skxyz->soxyz', tap_block, stacked, preferred_element_type=...]
  transfers between devices with their start and end apart: 13 -> 14, of which waited for: 7 -> 8; matrix products, arithmetic and copies ran while one was open for 2% -> 4% of each run, Pallas kernels for 0% -> 0%
where the time goes in v1:
time: 325 us; the launch traced here: 323 us
  waiting for transfers between devices  173 us (53%)
  blocking collectives  65.8 us (20%)
  matrix products  25.4 us (8%)
  starting transfers between devices  21.6 us (7%)
  between operations  14.6 us (4%)
  local copies, waits for them, and re-layouts  14 us (4%)
  other arithmetic  8.32 us (3%)
    psum x1, waiting for transfers between devices, one_after_other(): partial = lax.psum(array_2, first)  76.7 us
    psum x1, waiting for transfers between devices, one_after_other(): return lax.psum(partial, second)  60.2 us
    psum x1, blocking collectives, one_after_other(): partial = lax.psum(array_2, first)  41 us
    psum x1, blocking collectives, one_after_other(): return lax.psum(partial, second)  24.8 us
    ppermute x6, waiting for transfers between devices, extended(): after = lax.ppermute(initial, axis, down)  19.7 us
    ppermute x6, waiting for transfers between devices, extended(): before = lax.ppermute(last, axis, up)  16.3 us
    dot_general x18, matrix products, correlate(): jnp.einsum('soxyz,skxyz->ok', upstream, stacked, preferred_element_type=j...  12.7 us
    dot_general x27, matrix products, convolve(): jnp.einsum('ok,skxyz->soxyz', tap_block, stacked, preferred_element_type=...  12.6 us
  transfers between devices with their start and end apart: 14, of which 8 were waited for; matrix products, arithmetic and copies ran while one was open for 4% of the time, Pallas kernels for 0%

profile of v1, /device:TPU:1, one launch (start us, length us, event | category | flops | bytes accessed | tf_op | source)
XLA Modules:
  0.0 322.7 jit_solution(10904312133715604605)
XLA Ops:
  7.2 1.1 copy.113
  8.3 4.7 %collective-permute-start.9 = (bf16[1,32,1,8,128]{4,1,3,2,0:T(8,128)(2,1)S(1)}, bf16[1,32,1,8,128]{4,1,3,2,0:T(8,128)(2,1)S(1)}, u32[]{:S(2)}, u32[]{:S(2)}) collective-permute-start(bf16[1,32,1,8,128]{4,1,3,2,0:T(8,128)(2,1)S(1)} %get-tuple-element.109), channel_id=1, source_target_pairs={{2,0},{4,2},{6,4},{8,6},{10,8},{12,10},{14,12},{0,14},{3,1},{5,3},... | collective-permute-start | bytes 196616 | tf_op jit(solution)/shard_map/ppermute | solution.py:20
  13.1 1.1 copy.88
  14.2 3.6 %collective-permute-start.1 = (bf16[1,32,1,8,128]{4,1,3,2,0:T(8,128)(2,1)S(1)}, bf16[1,32,1,8,128]{4,1,3,2,0:T(8,128)(2,1)S(1)}, u32[]{:S(2)}, u32[]{:S(2)}) collective-permute-start(bf16[1,32,1,8,128]{4,1,3,2,0:T(8,128)(2,1)S(1)} %get-tuple-element.113), channel_id=1, source_target_pairs={{2,0},{4,2},{6,4},{8,6},{10,8},{12,10},{14,12},{0,14},{3,1},{5,3},... | collective-permute-start | bytes 196616 | tf_op jit(solution)/shard_map/ppermute | solution.py:20
  17.8 0.3 convert_reduce_fusion
  20.6 2.4 collective-permute-done
  23.1 3.4 %collective-permute-start.10 = (bf16[1,32,7,8,1]{4,1,3,2,0:T(8,128)(2,1)S(1)}, bf16[1,32,7,8,1]{4,1,3,2,0:T(8,128)(2,1)S(1)}, u32[]{:S(2)}, u32[]{:S(2)}) collective-permute-start(bf16[1,32,7,8,1]{4,1,3,2,0:T(8,128)(2,1)S(1)} %get-tuple-element.93), channel_id=1, source_target_pairs={{0,1},{1,0},{2,3},{3,2},{4,5},{5,4},{6,7},{7,6},{8,9},{9,8},{10,11... | collective-permute-start | bytes 10760 | tf_op jit(solution)/shard_map/ppermute | solution.py:19
  26.8 3.0 collective-permute-start.2
  29.8 4.7 %collective-permute-done.10 = bf16[1,32,7,8,1]{4,1,3,2,0:T(8,128)(2,1)S(1)} collective-permute-done((bf16[1,32,7,8,1]{4,1,3,2,0:T(8,128)(2,1)S(1)}, bf16[1,32,7,8,1]{4,1,3,2,0:T(8,128)(2,1)S(1)}, u32[]{:S(2)}, u32[]{:S(2)}) %collective-permute-start.10) | collective-permute-done | bytes 3616 | tf_op jit(solution)/shard_map/ppermute | solution.py:19
  34.5 9.8 %collective-permute-done.11 = bf16[1,32,7,8,1]{4,1,3,2,0:T(8,128)(2,1)S(1)} collective-permute-done((bf16[1,32,7,8,1]{4,1,3,2,0:T(8,128)(2,1)S(1)}, bf16[1,32,7,8,1]{4,1,3,2,0:T(8,128)(2,1)S(1)}, u32[]{:S(2)}, u32[]{:S(2)}) %collective-permute-start.11) | collective-permute-done | bytes 3616 | tf_op jit(solution)/shard_map/ppermute | solution.py:20
  44.4 0.6 select_maximum_fusion
  44.9 1.5 fusion.148
  46.5 7.7 %collective-permute-done.2 = bf16[1,32,7,8,1]{4,1,3,2,0:T(8,128)(2,1)S(1)} collective-permute-done((bf16[1,32,7,8,1]{4,1,3,2,0:T(8,128)(2,1)S(1)}, bf16[1,32,7,8,1]{4,1,3,2,0:T(8,128)(2,1)S(1)}, u32[]{:S(2)}, u32[]{:S(2)}) %collective-permute-start.2) | collective-permute-done | bytes 3616 | tf_op jit(solution)/shard_map/ppermute | solution.py:19
  54.2 9.8 %collective-permute-done.3 = bf16[1,32,7,8,1]{4,1,3,2,0:T(8,128)(2,1)S(1)} collective-permute-done((bf16[1,32,7,8,1]{4,1,3,2,0:T(8,128)(2,1)S(1)}, bf16[1,32,7,8,1]{4,1,3,2,0:T(8,128)(2,1)S(1)}, u32[]{:S(2)}, u32[]{:S(2)}) %collective-permute-start.3) | collective-permute-done | bytes 3616 | tf_op jit(solution)/shard_map/ppermute | solution.py:20
  64.0 0.6 fusion.20
  64.6 1.5 fusion.150
  66.4 0.6 fusion.101
  67.1 1.1 pad_maximum_fusion.14
  70.7 0.4 copy-done.5
  71.1 0.3 multiply_convert_fusion
  71.8 0.6 fusion.97
  72.4 0.3 convolution_add_fusion.7
  72.7 0.3 convolution_add_fusion.6
  73.0 0.3 convolution_add_fusion.5
  73.4 0.3 convolution_add_fusion.4
  74.3 1.0 convolution_add_fusion.1
  75.4 0.6 convert_reduce_fusion.1
  75.9 0.7 convolution_bitcast_fusion.6
  76.6 0.7 convolution_bitcast_fusion.5
  77.3 0.7 convolution_bitcast_fusion.4
  78.1 0.7 convolution_bitcast_fusion.3
  78.8 0.7 convolution_bitcast_fusion.1
  79.5 0.7 convolution_bitcast_fusion.7
  80.2 0.7 convolution_bitcast_fusion.8
  80.9 0.7 convolution_bitcast_fusion.2
  81.6 0.7 convolution_bitcast_fusion
  82.5 3.6 %collective-permute-start.5 = (bf16[1,32,1,8,128]{4,1,3,2,0:T(8,128)(2,1)S(1)}, bf16[1,32,1,8,128]{4,1,3,2,0:T(8,128)(2,1)S(1)}, u32[]{:S(2)}, u32[]{:S(2)}) collective-permute-start(bf16[1,32,1,8,128]{4,1,3,2,0:T(8,128)(2,1)S(1)} %get-tuple-element.112), channel_id=1, source_target_pairs={{2,0},{4,2},{6,4},{8,6},{10,8},{12,10},{14,12},{0,14},{3,1},{5,3},... | collective-permute-start | bytes 196616 | tf_op jit(solution)/shard_map/ppermute | solution.py:20
  86.1 1.6 collective-permute-done.4
  88.0 2.8 collective-permute-start.6
  91.0 0.8 maximum_multiply_fusion
  91.8 41.0 %all-reduce.3 = (f32[32]{0:T(128)S(1)}, f32[32]{0:T(128)S(1)}) all-reduce(f32[32]{0:T(128)S(1)} %broadcast_multiply_fusion.1, f32[32]{0:T(128)S(1)} %broadcast_multiply_fusion), channel_id=1, replica_groups=mesh['smp'=8,'gx'=8,'gz'=2] {'gx','gz'}, use_global_device_ids=true, to_apply=%region_3.4 | all-reduce | flops 64 | bytes 512 | tf_op jit(solution)/shard_map/psum | solution.py:8
  132.8 24.8 %all-reduce.5 = (f32[32]{0:T(128)}, f32[32]{0:T(128)}) all-reduce(f32[32]{0:T(128)S(1)} %get-tuple-element.15, f32[32]{0:T(128)S(1)} %get-tuple-element.16), channel_id=1, replica_groups=mesh['smp'=8,'gx'=8,'gz'=2] {'smp'}, use_global_device_ids=true, to_apply=%region_4.5 | all-reduce | flops 64 | bytes 512 | tf_op jit(solution)/shard_map/psum | solution.py:9
  157.6 0.7 maximum_maximum_fusion
  158.3 0.4 fusion.151
  159.1 0.7 convolution_bitcast_fusion.13
  159.8 0.7 convolution_bitcast_fusion.10
  160.5 0.7 convolution_bitcast_fusion.16
  161.2 0.6 select_maximum_fusion.2
  161.8 1.4 fusion.149
  163.4 0.7 convolution_bitcast_fusion.11
  164.1 0.7 convolution_bitcast_fusion.9
  165.0 0.7 convolution_bitcast_fusion.14
  165.7 0.7 convolution_bitcast_fusion.12
  166.9 0.7 convolution_bitcast_fusion.17
  167.6 0.7 convolution_bitcast_fusion.15
  169.7 1.1 convolution_add_fusion.10
  170.9 0.8 maximum_multiply_fusion.1
  171.8 2.2 convolution_add_fusion.9
  174.0 76.7 %all-reduce.10.cloned.1.call-done = (f32[32,3,3,3,32]{4,0,3,2,1:T(8,128)}, f32[32,3,3,3,32]{4,0,3,2,1:T(8,128)}) async-done(((f32[32,3,3,3,32]{4,0,3,2,1:T(8,128)}, f32[32,3,3,3,32]{4,0,3,2,1:T(8,128)}), (f32[32,3,3,3,32]{4,0,3,2,1:T(8,128)}, f32[32,3,3,3,32]{4,0,3,2,1:T(8,128)})) %all-reduce.10.cloned.1.call-update) | async-done | bytes 221200 | tf_op jit(solution)/shard_map/psum | solution.py:8
  250.8 1.4 fusion.12
  252.2 0.9 copy.164
  253.0 60.2 %all-reduce.12.cloned.1.call-done = (f32[32,3,3,3,32]{4,0,3,2,1:T(8,128)}, f32[32,3,3,3,32]{4,0,3,2,1:T(8,128)}) async-done(((f32[32,3,3,3,32]{4,0,3,2,1:T(8,128)}, f32[32,3,3,3,32]{4,0,3,2,1:T(8,128)}), (f32[32,3,3,3,32]{4,0,3,2,1:T(8,128)}, f32[32,3,3,3,32]{4,0,3,2,1:T(8,128)})) %all-reduce.12.cloned.1.call-update) | async-done | bytes 221200 | tf_op jit(solution)/shard_map/psum | solution.py:9
  313.2 1.9 copy.330
  315.1 0.8 copy.331
  (114 shorter events, 10.0 us)
Async XLA Ops:
  7.2 10.6 %copy-start = (bf16[1,32,5,8,128]{4,3,2,1,0:T(8,128)(2,1)S(1)}, bf16[1,32,5,8,128]{4,3,2,1,0:T(8,128)(2,1)}, u32[]{:S(2)}) copy-start(bf16[1,32,5,8,128]{4,3,2,1,0:T(8,128)(2,1)} %param.11) | copy-start | bytes 983044
  7.2 10.9 %copy-start.2 = (bf16[32,3,3,3,32]{4,0,3,2,1:T(8,128)(2,1)S(1)}, bf16[32,3,3,3,32]{4,0,3,2,1:T(8,128)(2,1)}, u32[]{:S(2)}) copy-start(bf16[32,3,3,3,32]{4,0,3,2,1:T(8,128)(2,1)} %param.9) | copy-start | bytes 165892
  7.2 243.6 %all-reduce.10.cloned.1.call-start = ((), (), s32[]{:S(2)}) async-start(), calls=%async_computation | async-start | bytes 1769472 | tf_op jit(solution)/shard_map/psum | solution.py:8
  8.3 12.0 %collective-permute-start.9 = (bf16[1,32,1,8,128]{4,1,3,2,0:T(8,128)(2,1)S(1)}, bf16[1,32,1,8,128]{4,1,3,2,0:T(8,128)(2,1)S(1)}, u32[]{:S(2)}, u32[]{:S(2)}) collective-permute-start(bf16[1,32,1,8,128]{4,1,3,2,0:T(8,128)(2,1)S(1)} %get-tuple-element.109), channel_id=1, source_target_pairs={{2,0},{4,2},{6,4},{8,6},{10,8},{12,10},{14,12},{0,14},{3,1},{5,3},... | collective-permute-start | bytes 196616 | tf_op jit(solution)/shard_map/ppermute | solution.py:20
  13.1 5.1 %copy-start.4 = (bf16[32,3,3,3,32]{4,0,3,2,1:T(8,128)(2,1)S(1)}, bf16[32,3,3,3,32]{4,0,3,2,1:T(8,128)(2,1)}, u32[]{:S(2)}) copy-start(bf16[32,3,3,3,32]{4,0,3,2,1:T(8,128)(2,1)} %param.7) | copy-start | bytes 165892
  13.1 7.2 %collective-permute-start.8 = (bf16[1,32,1,8,128]{4,1,3,2,0:T(8,128)(2,1)S(1)}, bf16[1,32,1,8,128]{4,1,3,2,0:T(8,128)(2,1)S(1)}, u32[]{:S(2)}, u32[]{:S(2)}) collective-permute-start(bf16[1,32,1,8,128]{4,1,3,2,0:T(8,128)(2,1)S(1)} %get-tuple-element.110), channel_id=1, source_target_pairs={{0,2},{2,4},{4,6},{6,8},{8,10},{10,12},{12,14},{14,0},{1,3},{3,5},... | collective-permute-start | bytes 196616 | tf_op jit(solution)/shard_map/ppermute | solution.py:19
  14.2 12.4 %collective-permute-start.1 = (bf16[1,32,1,8,128]{4,1,3,2,0:T(8,128)(2,1)S(1)}, bf16[1,32,1,8,128]{4,1,3,2,0:T(8,128)(2,1)S(1)}, u32[]{:S(2)}, u32[]{:S(2)}) collective-permute-start(bf16[1,32,1,8,128]{4,1,3,2,0:T(8,128)(2,1)S(1)} %get-tuple-element.113), channel_id=1, source_target_pairs={{2,0},{4,2},{6,4},{8,6},{10,8},{12,10},{14,12},{0,14},{3,1},{5,3},... | collective-permute-start | bytes 196616 | tf_op jit(solution)/shard_map/ppermute | solution.py:20
  17.8 5.2 %collective-permute-start = (bf16[1,32,1,8,128]{4,1,3,2,0:T(8,128)(2,1)S(1)}, bf16[1,32,1,8,128]{4,1,3,2,0:T(8,128)(2,1)S(1)}, u32[]{:S(2)}, u32[]{:S(2)}) collective-permute-start(bf16[1,32,1,8,128]{4,1,3,2,0:T(8,128)(2,1)S(1)} %get-tuple-element.114), channel_id=1, source_target_pairs={{0,2},{2,4},{4,6},{6,8},{8,10},{10,12},{12,14},{14,0},{1,3},{3,5},... | collective-permute-start | bytes 196616 | tf_op jit(solution)/shard_map/ppermute | solution.py:19
  20.3 2.7 copy-start.1
  23.1 11.4 %collective-permute-start.10 = (bf16[1,32,7,8,1]{4,1,3,2,0:T(8,128)(2,1)S(1)}, bf16[1,32,7,8,1]{4,1,3,2,0:T(8,128)(2,1)S(1)}, u32[]{:S(2)}, u32[]{:S(2)}) collective-permute-start(bf16[1,32,7,8,1]{4,1,3,2,0:T(8,128)(2,1)S(1)} %get-tuple-element.93), channel_id=1, source_target_pairs={{0,1},{1,0},{2,3},{3,2},{4,5},{5,4},{6,7},{7,6},{8,9},{9,8},{10,11... | collective-permute-start | bytes 10760 | tf_op jit(solution)/shard_map/ppermute | solution.py:19
  26.5 17.9 %collective-permute-start.11 = (bf16[1,32,7,8,1]{4,1,3,2,0:T(8,128)(2,1)S(1)}, bf16[1,32,7,8,1]{4,1,3,2,0:T(8,128)(2,1)S(1)}, u32[]{:S(2)}, u32[]{:S(2)}) collective-permute-start(bf16[1,32,7,8,1]{4,1,3,2,0:T(8,128)(2,1)S(1)} %get-tuple-element.94), channel_id=1, source_target_pairs={{1,0},{0,1},{3,2},{2,3},{5,4},{4,5},{7,6},{6,7},{9,8},{8,9},{11,10... | collective-permute-start | bytes 10760 | tf_op jit(solution)/shard_map/ppermute | solution.py:20
  26.8 27.4 %collective-permute-start.2 = (bf16[1,32,7,8,1]{4,1,3,2,0:T(8,128)(2,1)S(1)}, bf16[1,32,7,8,1]{4,1,3,2,0:T(8,128)(2,1)S(1)}, u32[]{:S(2)}, u32[]{:S(2)}) collective-permute-start(bf16[1,32,7,8,1]{4,1,3,2,0:T(8,128)(2,1)S(1)} %get-tuple-element.101), channel_id=1, source_target_pairs={{0,1},{1,0},{2,3},{3,2},{4,5},{5,4},{6,7},{7,6},{8,9},{9,8},{10,11... | collective-permute-start | bytes 10760 | tf_op jit(solution)/shard_map/ppermute | solution.py:19
  29.8 34.3 %collective-permute-start.3 = (bf16[1,32,7,8,1]{4,1,3,2,0:T(8,128)(2,1)S(1)}, bf16[1,32,7,8,1]{4,1,3,2,0:T(8,128)(2,1)S(1)}, u32[]{:S(2)}, u32[]{:S(2)}) collective-permute-start(bf16[1,32,7,8,1]{4,1,3,2,0:T(8,128)(2,1)S(1)} %get-tuple-element.102), channel_id=1, source_target_pairs={{1,0},{0,1},{3,2},{2,3},{5,4},{4,5},{7,6},{6,7},{9,8},{8,9},{11,10... | collective-permute-start | bytes 10760 | tf_op jit(solution)/shard_map/ppermute | solution.py:20
  70.5 0.7 copy-start.5
  82.4 5.3 %collective-permute-start.4 = (bf16[1,32,1,8,128]{4,1,3,2,0:T(8,128)(2,1)S(1)}, bf16[1,32,1,8,128]{4,1,3,2,0:T(8,128)(2,1)S(1)}, u32[]{:S(2)}, u32[]{:S(2)}) collective-permute-start(bf16[1,32,1,8,128]{4,1,3,2,0:T(8,128)(2,1)S(1)} %get-tuple-element.111), channel_id=1, source_target_pairs={{0,2},{2,4},{4,6},{6,8},{8,10},{10,12},{12,14},{14,0},{1,3},{3,5},... | collective-permute-start | bytes 196616 | tf_op jit(solution)/shard_map/ppermute | solution.py:19
  82.5 5.2 %collective-permute-start.5 = (bf16[1,32,1,8,128]{4,1,3,2,0:T(8,128)(2,1)S(1)}, bf16[1,32,1,8,128]{4,1,3,2,0:T(8,128)(2,1)S(1)}, u32[]{:S(2)}, u32[]{:S(2)}) collective-permute-start(bf16[1,32,1,8,128]{4,1,3,2,0:T(8,128)(2,1)S(1)} %get-tuple-element.112), channel_id=1, source_target_pairs={{2,0},{4,2},{6,4},{8,6},{10,8},{12,10},{14,12},{0,14},{3,1},{5,3},... | collective-permute-start | bytes 196616 | tf_op jit(solution)/shard_map/ppermute | solution.py:20
  88.0 69.7 %collective-permute-start.6 = (bf16[1,32,7,8,1]{4,1,3,2,0:T(8,128)(2,1)S(1)}, bf16[1,32,7,8,1]{4,1,3,2,0:T(8,128)(2,1)S(1)}, u32[]{:S(2)}, u32[]{:S(2)}) collective-permute-start(bf16[1,32,7,8,1]{4,1,3,2,0:T(8,128)(2,1)S(1)} %get-tuple-element.97), channel_id=1, source_target_pairs={{0,1},{1,0},{2,3},{3,2},{4,5},{5,4},{6,7},{7,6},{8,9},{9,8},{10,11... | collective-permute-start | bytes 10760 | tf_op jit(solution)/shard_map/ppermute | solution.py:19
  90.7 66.9 %collective-permute-start.7 = (bf16[1,32,7,8,1]{4,1,3,2,0:T(8,128)(2,1)S(1)}, bf16[1,32,7,8,1]{4,1,3,2,0:T(8,128)(2,1)S(1)}, u32[]{:S(2)}, u32[]{:S(2)}) collective-permute-start(bf16[1,32,7,8,1]{4,1,3,2,0:T(8,128)(2,1)S(1)} %get-tuple-element.98), channel_id=1, source_target_pairs={{1,0},{0,1},{3,2},{2,3},{5,4},{4,5},{7,6},{6,7},{9,8},{8,9},{11,10... | collective-permute-start | bytes 10760 | tf_op jit(solution)/shard_map/ppermute | solution.py:20
  171.8 79.0 %copy-start.6 = (f32[32]{0:T(128)S(1)}, f32[32]{0:T(128)}, u32[]{:S(2)}) copy-start(f32[32]{0:T(128)} %param.10) | copy-start | bytes 388
  171.8 141.5 %all-reduce.12.cloned.1.call-start = ((), (), s32[]{:S(2)}) async-start(), calls=%async_computation.1 | async-start | bytes 1769472 | tf_op jit(solution)/shard_map/psum | solution.py:9
  313.2 1.9 copy-start.3
Sparse Core Ops, SparseCore 0:
  171.9 78.8 all-reduce.9
  253.3 59.9 all-reduce.11
